TPU v7x, 32 devices: a whole 2x2x4 slice. The times are simulated.
32 devices in a mesh: pts: 16 (over z, x, core), proto: 2 (over y).
Axes of the slice: x: 2, y: 2, z: 4, core: 2. Of those that a mesh axis runs over, the one named last changes fastest.
Arguments:
- points: bfloat16 [128, 128, 1024], P('pts', None, 'proto'), as said below
- prototypes: bfloat16 [32, 512, 1024], P(('pts', 'proto')), as said below
- coarse_duals: float32 [32, 512], P(('pts', 'proto')), may hold values from -8 to 8
- active: int32 [128, 8], P('pts'), may hold values from 0 to 31, as said below
Outputs:
- point_duals: float32 [128, 128], P('pts')
- new_duals: float32 [32, 512], P(('pts', 'proto'))
Inputs may be any that keep to these rules, and one draw needn't show every extreme that they name: `active`: each row names 8 different blocks. Block b belongs to owner group b // 2. The 8 rows of one index of pts name any one owner group at most 8 times, and exactly that often for 8 groups. Over all rows every owner group is named 64 times in all, every block at least once and at most 32 times, and in every owner group some block exactly 32 times. `points`: Real-valued embeddings. `prototypes`: Real-valued embeddings.
All inputs are finite; a program needn't handle non-finite values.
Results may differ from a plain program's by a relative error of at most 0.0003.
Values may be sent and summed in bfloat16 or wider, within the bound.
A program may use at most 128 MiB of HBM per device.

v0:
```python
import jax
import jax.numpy as jnp
from jax import lax
from jax.sharding import PartitionSpec as P

LOWEST = -1e30


def body(points, prototypes, coarse_duals, active):
    groups = lax.axis_size("pts")
    owners = lax.axis_size("proto")
    blocks, row_count, slice_width = points.shape
    active_width = active.shape[1]
    pair_total = blocks * active_width
    capacity = max(2, 2 * pair_total // groups)
    bucket_cap = 3 * pair_total // (owners + 4)
    slot_count = groups * capacity
    pair_ids = jnp.arange(pair_total, dtype=jnp.int32)
    slot_ids = jnp.arange(slot_count, dtype=jnp.int32)
    targets = active.reshape(pair_total)
    dest_group = targets // owners
    dest_local = targets % owners
    before = (dest_group[:, None] == dest_group[None, :]) & (pair_ids[None, :] < pair_ids[:, None])
    slot_of_pair = dest_group * capacity + jnp.sum(before.astype(jnp.int32), axis=1)
    slot_hits = slot_of_pair[None, :] == slot_ids[:, None]
    filled = jnp.any(slot_hits, axis=1)
    pair_of_slot = jnp.sum(jnp.where(slot_hits, pair_ids[None, :], 0), axis=1)
    block_of_slot = pair_of_slot // active_width
    send_tag = jnp.where(filled, dest_local[pair_of_slot], owners)
    outgoing = jnp.where(filled[:, None, None], points[block_of_slot], jnp.zeros((), points.dtype))
    arrived, arrived_tag = (
        lax.all_to_all(
            outgoing.reshape(groups, capacity, row_count, slice_width),
            "pts",
            split_axis=0,
            concat_axis=0,
            tiled=True,
        ),
        lax.all_to_all(
            send_tag.reshape(groups, capacity), "pts", split_axis=0, concat_axis=0, tiled=True
        ),
    )
    arrived = arrived.reshape(slot_count, row_count, slice_width)
    arrived_tag = arrived_tag.reshape(slot_count)
    occupied = arrived_tag < owners
    earlier_slots = (arrived_tag[None, :] == arrived_tag[:, None]) & (
        slot_ids[None, :] < slot_ids[:, None]
    )
    position = jnp.sum(earlier_slots.astype(jnp.int32), axis=1)
    bucket_code = jnp.where(occupied, arrived_tag * bucket_cap + position, owners * bucket_cap)
    bucket_ids = jnp.arange(owners * bucket_cap, dtype=jnp.int32)
    bucket_match = bucket_code[None, :] == bucket_ids[:, None]
    taken = jnp.any(bucket_match, axis=1)
    slot_of_bucket = jnp.sum(jnp.where(bucket_match, slot_ids[None, :], 0), axis=1)
    sectioned = jnp.where(
        taken[:, None, None], arrived[slot_of_bucket], jnp.zeros((), arrived.dtype)
    )
    resident = lax.all_to_all(
        sectioned.reshape(owners, bucket_cap, row_count, slice_width),
        "proto",
        split_axis=0,
        concat_axis=3,
        tiled=True,
    )
    resident = resident.reshape(bucket_cap, row_count, slice_width * owners)
    my_index = lax.axis_index("proto")
    my_taken = lax.dynamic_slice_in_dim(taken.reshape(owners, bucket_cap), my_index, 1, 0)[0]
    my_slot = lax.dynamic_slice_in_dim(slot_of_bucket.reshape(owners, bucket_cap), my_index, 1, 0)[
        0
    ]
    owned_block = prototypes[0]
    scores = jnp.einsum("hrd,cd->hrc", resident, owned_block, preferred_element_type=jnp.float32)
    shifted = scores + coarse_duals[0][None, None, :]
    row_peak = jnp.max(shifted, axis=2)
    row_mass = jnp.sum(jnp.exp(shifted - row_peak[:, :, None]), axis=2)
    all_peak, all_mass = (
        lax.all_gather(row_peak[None], "proto", axis=0, tiled=True),
        lax.all_gather(row_mass[None], "proto", axis=0, tiled=True),
    )
    all_peak = all_peak.reshape(owners * bucket_cap, row_count)
    all_mass = all_mass.reshape(owners * bucket_cap, row_count)
    lookup = jnp.where(occupied, bucket_code, 0)
    back_peak = jnp.where(occupied[:, None], all_peak[lookup], LOWEST)
    back_mass = jnp.where(occupied[:, None], all_mass[lookup], 0.0)
    got_peak, got_mass = (
        lax.all_to_all(
            back_peak.reshape(groups, capacity, row_count),
            "pts",
            split_axis=0,
            concat_axis=0,
            tiled=True,
        ),
        lax.all_to_all(
            back_mass.reshape(groups, capacity, row_count),
            "pts",
            split_axis=0,
            concat_axis=0,
            tiled=True,
        ),
    )
    pair_peak = got_peak.reshape(slot_count, row_count)[slot_of_pair].reshape(
        blocks, active_width, row_count
    )
    pair_mass = got_mass.reshape(slot_count, row_count)[slot_of_pair].reshape(
        blocks, active_width, row_count
    )
    peak = jnp.max(pair_peak, axis=1)
    mass = jnp.sum(pair_mass * jnp.exp(pair_peak - peak[:, None, :]), axis=1)
    point_duals = -(peak + jnp.log(mass))
    outgoing_duals = jnp.where(filled[:, None], point_duals[block_of_slot], 0.0)
    arrived_duals = lax.all_to_all(
        outgoing_duals.reshape(groups, capacity, row_count),
        "pts",
        split_axis=0,
        concat_axis=0,
        tiled=True,
    )
    my_duals = arrived_duals.reshape(slot_count, row_count)[my_slot]
    rescored = jnp.einsum(
        "hrd,cd->hrc",
        lax.optimization_barrier(resident),
        owned_block,
        preferred_element_type=jnp.float32,
    )
    column_arg = jnp.where(my_taken[:, None, None], rescored + my_duals[:, :, None], LOWEST)
    col_peak = jnp.max(column_arg, axis=(0, 1))
    col_mass = jnp.sum(jnp.exp(column_arg - col_peak[None, None, :]), axis=(0, 1))
    new_duals = -(col_peak + jnp.log(col_mass))
    return (point_duals, new_duals[None, :])


def solution(mesh):
    return jax.shard_map(
        body,
        mesh=mesh,
        in_specs=(
            P("pts", None, "proto"),
            P(("pts", "proto"), None, None),
            P(("pts", "proto"), None),
            P("pts", None),
        ),
        out_specs=(P("pts", None), P(("pts", "proto"), None)),
        check_vma=False,
    )
```

profile of v0, /device:TPU:0, one launch (start us, length us, event | category | flops | bytes accessed | tf_op | source)
XLA Modules:
  0.0 616.0 jit_solution(16729566166568876897)
XLA Ops:
  0.6 0.0 copy-start
  0.6 0.9 reshape.444
  1.5 0.2 convert_reduce_fusion.1
  1.7 0.1 select_reduce_fusion.1
  1.8 0.1 fusion.9
  1.9 1.2 gather_fusion
  3.2 0.7 select_n.191
  3.9 7.4 %all-to-all-start = ((s32[16,1,8]{2,1,0:T(1,128)}), s32[16,1,8]{2,1,0:T(1,128)S(1)}, u32[]{:S(2)}, u32[]{:S(2)}) async-start(s32[16,1,8]{2,1,0:T(1,128)} %bitcast.2), calls=%async_computation | async-start | bytes 16384 | tf_op jit(solution)/shard_map/all_to_all | solution.py:39
  11.2 0.1 broadcast_in_dim.142
  11.3 0.0 copy-done
  11.3 7.9 %gather_fusion.1 = bf16[128,128,512]{2,1,0:T(8,128)(2,1)} fusion(bf16[8,128,512]{2,1,0:T(8,128)(2,1)S(1)} %copy-done, s32[1024]{0:T(1024)S(1)} %get-tuple-element.14), kind=kCustom, calls=%fused_computation.1 | custom fusion | bytes 33554944 | tf_op jit(solution)/shard_map/gather | solution.py:30
  19.3 14.0 %broadcast_select_fusion = bf16[16,8,128,512]{3,2,1,0:T(8,128)(2,1)} fusion(bf16[16,8,128,512]{3,2,1,0:T(8,128)(2,1)} %bitcast.84, pred[16,8]{1,0:T(8,128)(4,1)S(1)} %broadcast_in_dim.142), kind=kLoop, calls=%fused_computation.9 | loop fusion | flops 8388608 | bytes 33554560 | tf_op jit(solution)/shard_map/jit(_where)/select_n | solution.py:30
  33.2 0.0 all-to-all-done
  33.3 6.1 all-to-all-start.1
  39.3 0.5 broadcast.412
  39.8 0.7 multiply_reduce_fusion
  40.5 0.1 reshape.445
  40.6 0.2 convert_reduce_fusion
  40.8 0.1 fusion.8
  40.9 0.1 broadcast_in_dim.140
  41.0 0.1 select_reduce_fusion
  41.2 294.9 %all-to-all-done.1 = bf16[16,8,128,512]{3,2,1,0:T(8,128)(2,1)} async-done(((bf16[16,8,128,512]{3,2,1,0:T(8,128)(2,1)}), bf16[16,8,128,512]{3,2,1,0:T(8,128)(2,1)}, u32[]{:S(2)}, u32[]{:S(2)}) %all-to-all-start.1) | async-done | bytes 16777248 | tf_op jit(solution)/shard_map/all_to_all | solution.py:32
  336.1 11.3 %gather_fusion.2 = bf16[64,128,512]{2,1,0:T(8,128)(2,1)} fusion(bf16[128,128,512]{2,1,0:T(8,128)(2,1)} %bitcast.6, s32[1024]{0:T(1024)S(1)} %pad_clamp_fusion.3), kind=kCustom, calls=%fused_computation.2 | custom fusion | bytes 16777472 | tf_op jit(solution)/shard_map/gather | solution.py:56
  347.4 7.2 %broadcast_select_fusion.1 = bf16[2,32,128,512]{3,2,1,0:T(8,128)(2,1)} fusion(bf16[2,32,128,512]{3,2,1,0:T(8,128)(2,1)} %bitcast.85, pred[2,32]{1,0:T(4,128)(4,1)S(1)} %broadcast_in_dim.140), kind=kLoop, calls=%fused_computation.13 | loop fusion | flops 4194304 | bytes 16777280 | tf_op jit(solution)/shard_map/jit(_where)/select_n | solution.py:55
  354.6 0.0 copy-start.3
  354.6 7.1 %all-to-all-start.2 = ((bf16[2,32,128,512]{3,2,1,0:T(8,128)(2,1)}), bf16[2,32,128,512]{3,2,1,0:T(8,128)(2,1)}, u32[]{:S(2)}, u32[]{:S(2)}) async-start(bf16[2,32,128,512]{3,2,1,0:T(8,128)(2,1)} %broadcast_select_fusion.1), calls=%async_computation.2 | async-start | bytes 16777216 | tf_op jit(solution)/shard_map/all_to_all | solution.py:58
  361.7 0.0 copy-done.3
  361.7 0.1 reshape.450
  361.8 0.1 copy.18
  361.8 0.1 copy.21
  361.9 0.1 lt.144
  362.0 0.1 mul.54
  362.1 0.1 copy.19
  362.2 93.0 %all-to-all-done.2 = bf16[2,32,128,512]{3,2,1,0:T(8,128)(2,1)} async-done(((bf16[2,32,128,512]{3,2,1,0:T(8,128)(2,1)}), bf16[2,32,128,512]{3,2,1,0:T(8,128)(2,1)}, u32[]{:S(2)}, u32[]{:S(2)}) %all-to-all-start.2) | async-done | bytes 8388640 | tf_op jit(solution)/shard_map/all_to_all | solution.py:58
  455.2 16.4 %copy.20 = bf16[1,32,128,2,512]{4,3,2,1,0:T(2,128)(2,1)} copy(bf16[1,32,128,2,512]{4,2,1,3,0:T(8,128)(2,1)} %bitcast.11) | data formatting | bytes 16777216 | tf_op jit(solution)/shard_map/all_to_all | solution.py:58
  471.6 14.3 %reshape.447 = bf16[32,128,1024]{2,1,0:T(8,128)(2,1)} reshape(bf16[1,32,128,2,512]{4,3,2,1,0:T(2,128)(2,1)} %copy.20) | data formatting | bytes 16777216 | tf_op jit(solution)/shard_map/reshape | solution.py:65
  485.9 0.0 copy-done.4
  485.9 0.0 copy-done.5
  485.9 7.3 %add_reduce_fusion = (f32[32,128]{1,0:T(8,128)S(1)}, f32[32,128,512]{2,1,0:T(8,128)S(1)}) fusion(f32[512]{0:T(512)S(1)} %bitcast.89, bf16[32,128,1024]{2,1,0:T(8,128)(2,1)} %reshape.447, bf16[1,512,1024]{2,1,0:T(8,128)(2,1)S(1)} %copy-done.5), kind=kOutput, calls=%fused_computation.14 | convolution fusion | flops 4299157504 | bytes 17844224 | tf_op jit(solution)/shard_map/hrd,cd->hrc/dot_general | solution.py:72
  493.2 4.4 all-gather
  497.6 2.0 exponential_reduce_fusion.1
  499.7 4.4 all-gather.1
  504.1 0.6 gather_fusion.5
  504.7 0.6 gather_fusion.3
  505.4 0.7 bitcast_select_fusion.1
  506.1 69.7 %all-to-all-start.3 = ((f32[16,8,128]{2,1,0:T(8,128)}), f32[16,8,128]{2,1,0:T(8,128)S(1)}, u32[]{:S(2)}, u32[]{:S(2)}) async-start(f32[16,8,128]{2,1,0:T(8,128)} %get-tuple-element.5), calls=%async_computation.3 | async-start | bytes 131072 | tf_op jit(solution)/shard_map/all_to_all | solution.py:86
  575.9 6.9 %all-to-all-done.3 = f32[16,8,128]{2,1,0:T(8,128)S(1)} async-done(((f32[16,8,128]{2,1,0:T(8,128)}), f32[16,8,128]{2,1,0:T(8,128)S(1)}, u32[]{:S(2)}, u32[]{:S(2)}) %all-to-all-start.3) | async-done | bytes 65568 | tf_op jit(solution)/shard_map/all_to_all | solution.py:86
  582.8 3.5 all-to-all-start.4
  586.3 0.1 reshape.456
  586.4 0.6 gather_fusion.4
  587.0 6.1 all-to-all-done.4
  593.1 0.6 gather_fusion.6
  593.8 0.0 copy-start.2
  593.8 0.6 gather_fusion.7
  594.4 0.7 bitcast_select_fusion
  595.1 3.7 all-to-all-start.5
  598.8 6.6 %all-to-all-done.5 = f32[16,8,128]{2,1,0:T(8,128)S(1)} async-done(((f32[16,8,128]{2,1,0:T(8,128)}), f32[16,8,128]{2,1,0:T(8,128)S(1)}, u32[]{:S(2)}, u32[]{:S(2)}) %all-to-all-start.5) | async-done | bytes 65568 | tf_op jit(solution)/shard_map/all_to_all | solution.py:111
  605.5 0.6 gather_fusion.8
  606.1 0.0 copy-start.1
  606.1 7.4 %fusion = (f32[512]{0:T(512)S(1)}, f32[32,128,512]{2,1,0:T(8,128)S(1)}) fusion(f32[32,128]{1,0:T(8,128)S(1)} %gather_fusion.8, pred[32]{0:T(512)(128)(4,1)S(1)} %dynamic-slice_bitcast_fusion, bf16[32,128,1024]{2,1,0:T(8,128)(2,1)} %reshape.447, bf16[1,512,1024]{2,1,0:T(8,128)(2,1)S(1)} %copy-done.5), kind=kOutput, calls=%fused_computation.15 | convolution fusion | flops 4301258240 | bytes 17844256 | tf_op jit(solution)/shard_map/hrd,cd->hrc/dot_general | solution.py:119
  613.5 0.0 copy-done.2
  613.5 1.9 exponential_reduce_fusion
  615.4 0.6 add_negate_fusion.1
  616.0 0.0 copy-done.1
  (22 shorter events, 0.2 us)
Async XLA Ops:
  0.6 10.7 %copy-start = (bf16[8,128,512]{2,1,0:T(8,128)(2,1)S(1)}, bf16[8,128,512]{2,1,0:T(8,128)(2,1)}, u32[]{:S(2)}) copy-start(bf16[8,128,512]{2,1,0:T(8,128)(2,1)} %param.4) | copy-start | bytes 3145732
  3.9 29.4 %all-to-all-start = ((s32[16,1,8]{2,1,0:T(1,128)}), s32[16,1,8]{2,1,0:T(1,128)S(1)}, u32[]{:S(2)}, u32[]{:S(2)}) async-start(s32[16,1,8]{2,1,0:T(1,128)} %bitcast.2), calls=%async_computation | async-start | bytes 16384 | tf_op jit(solution)/shard_map/all_to_all | solution.py:39
  33.3 302.8 %all-to-all-start.1 = ((bf16[16,8,128,512]{3,2,1,0:T(8,128)(2,1)}), bf16[16,8,128,512]{3,2,1,0:T(8,128)(2,1)}, u32[]{:S(2)}, u32[]{:S(2)}) async-start(bf16[16,8,128,512]{3,2,1,0:T(8,128)(2,1)} %broadcast_select_fusion), calls=%async_computation.1 | async-start | bytes 33554432 | tf_op jit(solution)/shard_map/all_to_all | solution.py:32
  354.6 7.1 %copy-start.3 = (s32[8,8]{1,0:T(8,128)S(1)}, s32[8,8]{1,0:T(8,128)}, u32[]{:S(2)}) copy-start(s32[8,8]{1,0:T(8,128)} %param.7) | copy-start | bytes 772
  354.6 100.6 %all-to-all-start.2 = ((bf16[2,32,128,512]{3,2,1,0:T(8,128)(2,1)}), bf16[2,32,128,512]{3,2,1,0:T(8,128)(2,1)}, u32[]{:S(2)}, u32[]{:S(2)}) async-start(bf16[2,32,128,512]{3,2,1,0:T(8,128)(2,1)} %broadcast_select_fusion.1), calls=%async_computation.2 | async-start | bytes 16777216 | tf_op jit(solution)/shard_map/all_to_all | solution.py:58
  471.6 14.4 %copy-start.4 = (f32[1,512]{1,0:T(1,128)S(1)}, f32[1,512]{1,0:T(1,128)}, u32[]{:S(2)}) copy-start(f32[1,512]{1,0:T(1,128)} %param.6) | copy-start | bytes 6148
  471.6 14.4 %copy-start.5 = (bf16[1,512,1024]{2,1,0:T(8,128)(2,1)S(1)}, bf16[1,512,1024]{2,1,0:T(8,128)(2,1)}, u32[]{:S(2)}) copy-start(bf16[1,512,1024]{2,1,0:T(8,128)(2,1)} %param.5) | copy-start | bytes 3145732
  506.1 76.6 %all-to-all-start.3 = ((f32[16,8,128]{2,1,0:T(8,128)}), f32[16,8,128]{2,1,0:T(8,128)S(1)}, u32[]{:S(2)}, u32[]{:S(2)}) async-start(f32[16,8,128]{2,1,0:T(8,128)} %get-tuple-element.5), calls=%async_computation.3 | async-start | bytes 131072 | tf_op jit(solution)/shard_map/all_to_all | solution.py:86
  582.8 10.4 %all-to-all-start.4 = ((f32[16,8,128]{2,1,0:T(8,128)}), f32[16,8,128]{2,1,0:T(8,128)S(1)}, u32[]{:S(2)}, u32[]{:S(2)}) async-start(f32[16,8,128]{2,1,0:T(8,128)} %get-tuple-element.4), calls=%async_computation.4 | async-start | bytes 131072 | tf_op jit(solution)/shard_map/all_to_all | solution.py:93
  593.8 19.7 %copy-start.2 = (f32[8,128]{1,0:T(8,128)}, f32[8,128]{1,0:T(8,128)S(1)}, u32[]{:S(2)}) copy-start(f32[8,128]{1,0:T(8,128)S(1)} %add_negate_fusion) | copy-start | bytes 12292
  595.1 10.4 %all-to-all-start.5 = ((f32[16,8,128]{2,1,0:T(8,128)}), f32[16,8,128]{2,1,0:T(8,128)S(1)}, u32[]{:S(2)}, u32[]{:S(2)}) async-start(f32[16,8,128]{2,1,0:T(8,128)} %bitcast_select_fusion), calls=%async_computation.5 | async-start | bytes 131072 | tf_op jit(solution)/shard_map/all_to_all | solution.py:111
  606.1 9.9 %copy-start.1 = (bf16[8,128,512]{2,1,0:T(8,128)(2,1)S(1)}, bf16[8,128,512]{2,1,0:T(8,128)(2,1)}, u32[]{:S(2)}) copy-start(bf16[8,128,512]{2,1,0:T(8,128)(2,1)} %param.4) | copy-start | bytes 3145732
where the time goes:
time: 617 us; the launch traced here: 616 us
  waiting for transfers between devices  408 us (66%)
  starting transfers between devices  97.4 us (16%)
  local copies, waits for them, and re-layouts  57.8 us (9%)
  other arithmetic  28.8 us (5%)
  matrix products  14.7 us (2%)
  blocking collectives  8.83 us (1%)
    all_to_all x1, waiting for transfers between devices, body(): lax.all_to_all(outgoing.reshape(groups, capacity, row_count, slice_width)...  295 us
    all_to_all x1, waiting for transfers between devices, body(): lax.all_to_all(sectioned.reshape(owners, bucket_cap, row_count, slice_wid...  93 us
    all_to_all x1, starting transfers between devices, body(): lax.all_to_all(back_peak.reshape(groups, capacity, row_count), 'pts', spl...  69.7 us
    all_to_all x1, local copies, waits for them, and re-layouts, body(): lax.all_to_all(sectioned.reshape(owners, bucket_cap, row_count, slice_wid...  16.4 us
    reshape x1, local copies, waits for them, and re-layouts, body(): resident = resident.reshape(bucket_cap, row_count, slice_width * owners)  14.3 us
    select_n x1, other arithmetic, body(): jnp.where(filled[:, None, None], points[block_of_slot], jnp.zeros((), poi...  14 us
  transfers between devices with their start and end apart: 6, of which 5 were waited for; matrix products, arithmetic and copies ran while one was open for 4% of the time, Pallas kernels for 0%

commit v1 on v0

--- a/solution.py
+++ b/solution.py
@@ -4,6 +4,22 @@
 from jax.sharding import PartitionSpec as P
 
 LOWEST = -1e30
+
+
+def swapped_with_each(array, axis, split, join):
+    ways, here = (lax.axis_size(axis), lax.axis_index(axis))
+    width = array.shape[split] // ways
+    shape = list(array.shape)
+    shape[split] = width
+    height = shape[join]
+    shape[join] = height * ways
+    full = jnp.zeros(shape, array.dtype)
+    for mask in range(ways):
+        part = lax.dynamic_slice_in_dim(array, (here ^ mask) * width, width, axis=split)
+        if mask:
+            part = lax.ppermute(part, axis, [(d, d ^ mask) for d in range(ways)])
+        full = lax.dynamic_update_slice_in_dim(full, part, (here ^ mask) * height, axis=join)
+    return full
 
 
 def body(points, prototypes, coarse_duals, active):
@@ -29,13 +45,7 @@
     send_tag = jnp.where(filled, dest_local[pair_of_slot], owners)
     outgoing = jnp.where(filled[:, None, None], points[block_of_slot], jnp.zeros((), points.dtype))
     arrived, arrived_tag = (
-        lax.all_to_all(
-            outgoing.reshape(groups, capacity, row_count, slice_width),
-            "pts",
-            split_axis=0,
-            concat_axis=0,
-            tiled=True,
-        ),
+        swapped_with_each(outgoing.reshape(groups, capacity, row_count, slice_width), "pts", 0, 0),
         lax.all_to_all(
             send_tag.reshape(groups, capacity), "pts", split_axis=0, concat_axis=0, tiled=True
         ),

time: 617 us -> 666 us (1.079)
  waiting for transfers between devices: 408 us -> 352 us
  blocking collectives: 8.83 us -> 57.2 us
  local copies, waits for them, and re-layouts: 57.8 us -> 96.5 us
  starting transfers between devices: 97.4 us -> 121 us
    all_to_all x2 -> x0, waiting for transfers between devices: 295 us -> none  [the longest x1 295 us: body(): lax.all_to_all(outgoing.reshape(groups, capacity, row_count, slice_width)...]
    ppermute x0 -> x15, waiting for transfers between devices: none -> 239 us  [swapped_with_each(): part = lax.ppermute(part, axis, [(d, d ^ mask) for d in range(ways)])]
    all_to_all x0 -> x1, blocking collectives: none -> 48.2 us  [body(): lax.all_to_all(send_tag.reshape(groups, capacity), 'pts', split_axis=0, c...]
    dynamic_update_slice x0 -> x15, local copies, waits for them, and re-layouts: none -> 28.4 us  [swapped_with_each(): lax.dynamic_update_slice_in_dim(full, part, (here ^ mask) * height, axis=...]
    ppermute x0 -> x15, starting transfers between devices: none -> 18.7 us  [swapped_with_each(): part = lax.ppermute(part, axis, [(d, d ^ mask) for d in range(ways)])]
    all_to_all x1, starting transfers between devices: 69.7 us -> 88.3 us  [body(): lax.all_to_all(back_peak.reshape(groups, capacity, row_count), 'pts', spl...]
    all_to_all x2 -> x0, starting transfers between devices: 13.4 us -> none  [the longest x1 7.36 us: body(): lax.all_to_all(send_tag.reshape(groups, capacity), 'pts', split_axis=0, c...]
  transfers between devices with their start and end apart: 6 -> 19, of which waited for: 5 -> 9; matrix products, arithmetic and copies ran while one was open for 4% -> 5% of each run, Pallas kernels for 0% -> 0%
where the time goes in v1:
time: 666 us; the launch traced here: 665 us
  waiting for transfers between devices  352 us (53%)
  starting transfers between devices  121 us (18%)
  local copies, waits for them, and re-layouts  96.5 us (14%)
  blocking collectives  57.2 us (9%)
  other arithmetic  23.1 us (3%)
  matrix products  14.7 us (2%)
    ppermute x15, waiting for transfers between devices, swapped_with_each(): part = lax.ppermute(part, axis, [(d, d ^ mask) for d in range(ways)])  239 us
    all_to_all x1, waiting for transfers between devices, body(): lax.all_to_all(sectioned.reshape(owners, bucket_cap, row_count, slice_wid...  92.3 us
    all_to_all x1, starting transfers between devices, body(): lax.all_to_all(back_peak.reshape(groups, capacity, row_count), 'pts', spl...  88.3 us
    all_to_all x1, blocking collectives, body(): lax.all_to_all(send_tag.reshape(groups, capacity), 'pts', split_axis=0, c...  48.2 us
    dynamic_update_slice x15, local copies, waits for them, and re-layouts, swapped_with_each(): lax.dynamic_update_slice_in_dim(full, part, (here ^ mask) * height, axis=...  28.4 us
    ppermute x15, starting transfers between devices, swapped_with_each(): part = lax.ppermute(part, axis, [(d, d ^ mask) for d in range(ways)])  18.7 us
    all_to_all x1, local copies, waits for them, and re-layouts, body(): lax.all_to_all(sectioned.reshape(owners, bucket_cap, row_count, slice_wid...  16.5 us
    reshape x1, local copies, waits for them, and re-layouts, body(): resident = resident.reshape(bucket_cap, row_count, slice_width * owners)  14.2 us
  transfers between devices with their start and end apart: 19, of which 9 were waited for; matrix products, arithmetic and copies ran while one was open for 5% of the time, Pallas kernels for 0%

profile of v1, /device:TPU:0, one launch (start us, length us, event | category | flops | bytes accessed | tf_op | source)
XLA Modules:
  0.0 665.2 jit_solution(2263288871396586030)
XLA Ops:
  0.7 0.8 reshape.444
  2.2 7.9 %gather_fusion.1 = bf16[128,128,512]{2,1,0:T(8,128)(2,1)} fusion(bf16[8,128,512]{2,1,0:T(8,128)(2,1)S(1)} %copy-done, s32[1024]{0:T(1024)S(1)} %get-tuple-element.30), kind=kCustom, calls=%fused_computation.1 | custom fusion | bytes 33554944 | tf_op jit(solution)/shard_map/gather | solution.py:46
  10.1 8.3 %broadcast_select_fusion = bf16[16,8,128,512]{3,2,1,0:T(8,128)(2,1)S(1)} fusion(bf16[16,8,128,512]{3,2,1,0:T(8,128)(2,1)} %bitcast.86, pred[16,8]{1,0:T(8,128)(4,1)S(1)} %broadcast_in_dim.144), kind=kLoop, calls=%fused_computation.9 | loop fusion | flops 8388608 | bytes 33554560 | tf_op jit(solution)/shard_map/jit(_where)/select_n | solution.py:46
  18.4 5.9 broadcast_in_dim.143
  24.3 4.9 constant_dynamic-slice_fusion.1
  29.8 2.3 collective-permute-start.1
  32.2 2.0 collective-permute-start.3
  34.2 1.2 gather_fusion
  35.5 48.2 %all_to_all.36 = s32[16,1,8]{2,1,0:T(1,128)S(1)} all-to-all(s32[16,1,8]{2,1,0:T(1,128)S(1)} %bitcast.92), channel_id=1, replica_groups=mesh['pts'=16,'proto'=2] {'pts'}, dimensions={0} | all-to-all | bytes 1024 | tf_op jit(solution)/shard_map/all_to_all | solution.py:49
  84.3 0.7 multiply_reduce_fusion
  85.2 0.6 collective-permute-start.5
  85.9 1.5 collective-permute-start.6
  87.4 0.6 collective-permute-start.7
  88.1 2.7 collective-permute-start.8
  91.6 2.3 constant_dynamic-update-slice_fusion.14
  93.9 2.3 constant_dynamic-update-slice_fusion.13
  96.2 58.2 %collective-permute-done.5 = bf16[1,8,128,512]{3,2,1,0:T(8,128)(2,1)} collective-permute-done((bf16[1,8,128,512]{3,2,1,0:T(8,128)(2,1)}, bf16[1,8,128,512]{3,2,1,0:T(8,128)(2,1)}, u32[]{:S(2)}, u32[]{:S(2)}) %collective-permute-start.5) | collective-permute-done | bytes 1048608 | tf_op jit(solution)/shard_map/ppermute | solution.py:20
  154.3 2.3 constant_dynamic-update-slice_fusion.12
  156.6 17.8 %collective-permute-done.6 = bf16[1,8,128,512]{3,2,1,0:T(8,128)(2,1)} collective-permute-done((bf16[1,8,128,512]{3,2,1,0:T(8,128)(2,1)}, bf16[1,8,128,512]{3,2,1,0:T(8,128)(2,1)}, u32[]{:S(2)}, u32[]{:S(2)}) %collective-permute-start.6) | collective-permute-done | bytes 1048608 | tf_op jit(solution)/shard_map/ppermute | solution.py:20
  174.4 2.4 collective-permute-start.11
  176.8 2.3 constant_dynamic-update-slice_fusion.11
  179.0 2.1 collective-permute-start.12
  181.1 2.3 constant_dynamic-update-slice_fusion.10
  183.5 88.5 %collective-permute-done.8 = bf16[1,8,128,512]{3,2,1,0:T(8,128)(2,1)} collective-permute-done((bf16[1,8,128,512]{3,2,1,0:T(8,128)(2,1)}, bf16[1,8,128,512]{3,2,1,0:T(8,128)(2,1)}, u32[]{:S(2)}, u32[]{:S(2)}) %collective-permute-start.8) | collective-permute-done | bytes 1048608 | tf_op jit(solution)/shard_map/ppermute | solution.py:20
  272.0 1.2 collective-permute-start.13
  273.2 2.3 constant_dynamic-update-slice_fusion.9
  275.5 41.4 %collective-permute-done.9 = bf16[1,8,128,512]{3,2,1,0:T(8,128)(2,1)} collective-permute-done((bf16[1,8,128,512]{3,2,1,0:T(8,128)(2,1)}, bf16[1,8,128,512]{3,2,1,0:T(8,128)(2,1)}, u32[]{:S(2)}, u32[]{:S(2)}) %collective-permute-start.9) | collective-permute-done | bytes 1048608 | tf_op jit(solution)/shard_map/ppermute | solution.py:20
  316.9 2.1 collective-permute-start.14
  319.0 2.3 constant_dynamic-update-slice_fusion.8
  321.3 2.4 constant_dynamic-update-slice_fusion.7
  323.6 2.3 constant_dynamic-update-slice_fusion.6
  325.9 2.3 constant_dynamic-update-slice_fusion.5
  328.2 33.5 %collective-permute-done.10 = bf16[1,8,128,512]{3,2,1,0:T(8,128)(2,1)S(1)} collective-permute-done((bf16[1,8,128,512]{3,2,1,0:T(8,128)(2,1)}, bf16[1,8,128,512]{3,2,1,0:T(8,128)(2,1)S(1)}, u32[]{:S(2)}, u32[]{:S(2)}) %collective-permute-start.10) | collective-permute-done | bytes 1048608 | tf_op jit(solution)/shard_map/ppermute | solution.py:20
  361.7 1.1 constant_dynamic-update-slice_fusion.4
  362.8 1.2 constant_dynamic-update-slice_fusion.3
  364.0 1.1 constant_dynamic-update-slice_fusion.2
  365.0 1.1 constant_dynamic-update-slice_fusion.1
  366.1 1.1 constant_dynamic-update-slice_fusion
  367.2 11.3 %gather_fusion.2 = bf16[64,128,512]{2,1,0:T(8,128)(2,1)} fusion(bf16[128,128,512]{2,1,0:T(8,128)(2,1)} %bitcast.87, s32[1024]{0:T(1024)S(1)} %pad_clamp_fusion.3), kind=kCustom, calls=%fused_computation.2 | custom fusion | bytes 16777472 | tf_op jit(solution)/shard_map/gather | solution.py:66
  378.6 7.2 %broadcast_select_fusion.1 = bf16[2,32,128,512]{3,2,1,0:T(8,128)(2,1)} fusion(bf16[2,32,128,512]{3,2,1,0:T(8,128)(2,1)} %bitcast.88, pred[2,32]{1,0:T(4,128)(4,1)S(1)} %broadcast_in_dim.141), kind=kLoop, calls=%fused_computation.13 | loop fusion | flops 4194304 | bytes 16777280 | tf_op jit(solution)/shard_map/jit(_where)/select_n | solution.py:65
  385.8 6.9 %all-to-all-start.1 = ((bf16[2,32,128,512]{3,2,1,0:T(8,128)(2,1)}), bf16[2,32,128,512]{3,2,1,0:T(8,128)(2,1)}, u32[]{:S(2)}, u32[]{:S(2)}) async-start(bf16[2,32,128,512]{3,2,1,0:T(8,128)(2,1)} %broadcast_select_fusion.1), calls=%async_computation.1 | async-start | bytes 16777216 | tf_op jit(solution)/shard_map/all_to_all | solution.py:68
  393.3 92.3 %all-to-all-done.1 = bf16[2,32,128,512]{3,2,1,0:T(8,128)(2,1)} async-done(((bf16[2,32,128,512]{3,2,1,0:T(8,128)(2,1)}), bf16[2,32,128,512]{3,2,1,0:T(8,128)(2,1)}, u32[]{:S(2)}, u32[]{:S(2)}) %all-to-all-start.1) | async-done | bytes 8388640 | tf_op jit(solution)/shard_map/all_to_all | solution.py:68
  485.6 16.5 %copy.20 = bf16[1,32,128,2,512]{4,3,2,1,0:T(2,128)(2,1)} copy(bf16[1,32,128,2,512]{4,2,1,3,0:T(8,128)(2,1)} %bitcast.11) | data formatting | bytes 16777216 | tf_op jit(solution)/shard_map/all_to_all | solution.py:68
  502.1 14.2 %reshape.447 = bf16[32,128,1024]{2,1,0:T(8,128)(2,1)} reshape(bf16[1,32,128,2,512]{4,3,2,1,0:T(2,128)(2,1)} %copy.20) | data formatting | bytes 16777216 | tf_op jit(solution)/shard_map/reshape | solution.py:75
  516.3 7.3 %add_reduce_fusion = (f32[32,128]{1,0:T(8,128)S(1)}, f32[32,128,512]{2,1,0:T(8,128)S(1)}) fusion(f32[512]{0:T(512)S(1)} %bitcast.93, bf16[32,128,1024]{2,1,0:T(8,128)(2,1)} %reshape.447, bf16[1,512,1024]{2,1,0:T(8,128)(2,1)S(1)} %copy-done.5), kind=kOutput, calls=%fused_computation.14 | convolution fusion | flops 4299157504 | bytes 17844224 | tf_op jit(solution)/shard_map/hrd,cd->hrc/dot_general | solution.py:82
  523.6 4.6 all-gather
  528.2 2.0 exponential_reduce_fusion.1
  530.2 4.4 all-gather.1
  534.7 0.6 gather_fusion.3
  535.3 0.6 gather_fusion.5
  535.9 0.7 bitcast_select_fusion.1
  536.7 88.3 %all-to-all-start.2 = ((f32[16,8,128]{2,1,0:T(8,128)}), f32[16,8,128]{2,1,0:T(8,128)S(1)}, u32[]{:S(2)}, u32[]{:S(2)}) async-start(f32[16,8,128]{2,1,0:T(8,128)} %get-tuple-element.21), calls=%async_computation.2 | async-start | bytes 131072 | tf_op jit(solution)/shard_map/all_to_all | solution.py:96
  625.1 6.9 %all-to-all-done.2 = f32[16,8,128]{2,1,0:T(8,128)S(1)} async-done(((f32[16,8,128]{2,1,0:T(8,128)}), f32[16,8,128]{2,1,0:T(8,128)S(1)}, u32[]{:S(2)}, u32[]{:S(2)}) %all-to-all-start.2) | async-done | bytes 65568 | tf_op jit(solution)/shard_map/all_to_all | solution.py:96
  631.9 3.5 all-to-all-start.3
  635.5 0.6 gather_fusion.4
  636.1 6.1 all-to-all-done.3
  642.3 0.6 gather_fusion.6
  642.9 0.6 gather_fusion.7
  643.6 0.7 bitcast_select_fusion
  644.3 3.5 all-to-all-start.4
  647.8 6.8 %all-to-all-done.4 = f32[16,8,128]{2,1,0:T(8,128)S(1)} async-done(((f32[16,8,128]{2,1,0:T(8,128)}), f32[16,8,128]{2,1,0:T(8,128)S(1)}, u32[]{:S(2)}, u32[]{:S(2)}) %all-to-all-start.4) | async-done | bytes 65568 | tf_op jit(solution)/shard_map/all_to_all | solution.py:121
  655.2 7.4 %fusion = (f32[512]{0:T(512)S(1)}, f32[32,128,512]{2,1,0:T(8,128)S(1)}) fusion(f32[32,128]{1,0:T(8,128)S(1)} %gather_fusion.8, pred[32]{0:T(512)(128)(4,1)S(1)} %fusion.11, bf16[32,128,1024]{2,1,0:T(8,128)(2,1)} %reshape.447, bf16[1,512,1024]{2,1,0:T(8,128)(2,1)S(1)} %copy-done.5), kind=kOutput, calls=%fused_computation.15 | convolution fusion | flops 4301258240 | bytes 17844256 | tf_op jit(solution)/shard_map/hrd,cd->hrc/dot_general | solution.py:129
  662.7 1.9 exponential_reduce_fusion
  664.6 0.6 add_negate_fusion.1
  (66 shorter events, 4.2 us)
Async XLA Ops:
  0.6 1.5 copy-start
  29.3 56.0 %collective-permute-start = (bf16[1,8,128,512]{3,2,1,0:T(8,128)(2,1)}, bf16[1,8,128,512]{3,2,1,0:T(8,128)(2,1)}, u32[]{:S(2)}, u32[]{:S(2)}) collective-permute-start(bf16[1,8,128,512]{3,2,1,0:T(8,128)(2,1)} %get-tuple-element.18), channel_id=1, source_target_pairs={{0,2},{2,0},{4,6},{6,4},{8,10},{10,8},{12,14},{14,12},{16,18},{18,... | collective-permute-start | bytes 3145736 | tf_op jit(solution)/shard_map/ppermute | solution.py:20
  29.8 56.0 %collective-permute-start.1 = (bf16[1,8,128,512]{3,2,1,0:T(8,128)(2,1)}, bf16[1,8,128,512]{3,2,1,0:T(8,128)(2,1)}, u32[]{:S(2)}, u32[]{:S(2)}) collective-permute-start(bf16[1,8,128,512]{3,2,1,0:T(8,128)(2,1)} %get-tuple-element.17), channel_id=1, source_target_pairs={{0,4},{2,6},{4,0},{6,2},{8,12},{10,14},{12,8},{14,10},{16,20},{18,... | collective-permute-start | bytes 3145736 | tf_op jit(solution)/shard_map/ppermute | solution.py:20
  32.2 55.2 %collective-permute-start.2 = (bf16[1,8,128,512]{3,2,1,0:T(8,128)(2,1)}, bf16[1,8,128,512]{3,2,1,0:T(8,128)(2,1)}, u32[]{:S(2)}, u32[]{:S(2)}) collective-permute-start(bf16[1,8,128,512]{3,2,1,0:T(8,128)(2,1)} %get-tuple-element.16), channel_id=1, source_target_pairs={{0,6},{2,4},{4,2},{6,0},{8,14},{10,12},{12,10},{14,8},{16,22},{18,... | collective-permute-start | bytes 3145736 | tf_op jit(solution)/shard_map/ppermute | solution.py:20
  32.2 55.8 %collective-permute-start.3 = (bf16[1,8,128,512]{3,2,1,0:T(8,128)(2,1)}, bf16[1,8,128,512]{3,2,1,0:T(8,128)(2,1)}, u32[]{:S(2)}, u32[]{:S(2)}) collective-permute-start(bf16[1,8,128,512]{3,2,1,0:T(8,128)(2,1)} %get-tuple-element.15), channel_id=1, source_target_pairs={{0,8},{2,10},{4,12},{6,14},{8,0},{10,2},{12,4},{14,6},{16,24},{18,... | collective-permute-start | bytes 3145736 | tf_op jit(solution)/shard_map/ppermute | solution.py:20
  34.2 56.6 %collective-permute-start.4 = (bf16[1,8,128,512]{3,2,1,0:T(8,128)(2,1)}, bf16[1,8,128,512]{3,2,1,0:T(8,128)(2,1)}, u32[]{:S(2)}, u32[]{:S(2)}) collective-permute-start(bf16[1,8,128,512]{3,2,1,0:T(8,128)(2,1)} %get-tuple-element.14), channel_id=1, source_target_pairs={{0,10},{2,8},{4,14},{6,12},{8,2},{10,0},{12,6},{14,4},{16,26},{18,... | collective-permute-start | bytes 3145736 | tf_op jit(solution)/shard_map/ppermute | solution.py:20
  85.2 69.1 %collective-permute-start.5 = (bf16[1,8,128,512]{3,2,1,0:T(8,128)(2,1)}, bf16[1,8,128,512]{3,2,1,0:T(8,128)(2,1)}, u32[]{:S(2)}, u32[]{:S(2)}) collective-permute-start(bf16[1,8,128,512]{3,2,1,0:T(8,128)(2,1)} %get-tuple-element.13), channel_id=1, source_target_pairs={{0,12},{2,14},{4,8},{6,10},{8,4},{10,6},{12,0},{14,2},{16,28},{18,... | collective-permute-start | bytes 3145736 | tf_op jit(solution)/shard_map/ppermute | solution.py:20
  85.9 88.5 %collective-permute-start.6 = (bf16[1,8,128,512]{3,2,1,0:T(8,128)(2,1)}, bf16[1,8,128,512]{3,2,1,0:T(8,128)(2,1)}, u32[]{:S(2)}, u32[]{:S(2)}) collective-permute-start(bf16[1,8,128,512]{3,2,1,0:T(8,128)(2,1)} %get-tuple-element.12), channel_id=1, source_target_pairs={{0,14},{2,12},{4,10},{6,8},{8,6},{10,4},{12,2},{14,0},{16,30},{18,... | collective-permute-start | bytes 3145736 | tf_op jit(solution)/shard_map/ppermute | solution.py:20
  87.4 91.7 %collective-permute-start.7 = (bf16[1,8,128,512]{3,2,1,0:T(8,128)(2,1)}, bf16[1,8,128,512]{3,2,1,0:T(8,128)(2,1)}, u32[]{:S(2)}, u32[]{:S(2)}) collective-permute-start(bf16[1,8,128,512]{3,2,1,0:T(8,128)(2,1)} %get-tuple-element.11), channel_id=1, source_target_pairs={{0,16},{2,18},{4,20},{6,22},{8,24},{10,26},{12,28},{14,30},{16,0},... | collective-permute-start | bytes 3145736 | tf_op jit(solution)/shard_map/ppermute | solution.py:20
  88.1 183.9 %collective-permute-start.8 = (bf16[1,8,128,512]{3,2,1,0:T(8,128)(2,1)}, bf16[1,8,128,512]{3,2,1,0:T(8,128)(2,1)}, u32[]{:S(2)}, u32[]{:S(2)}) collective-permute-start(bf16[1,8,128,512]{3,2,1,0:T(8,128)(2,1)} %get-tuple-element.10), channel_id=1, source_target_pairs={{0,18},{2,16},{4,22},{6,20},{8,26},{10,24},{12,30},{14,28},{16,2},... | collective-permute-start | bytes 3145736 | tf_op jit(solution)/shard_map/ppermute | solution.py:20
  90.8 226.1 %collective-permute-start.9 = (bf16[1,8,128,512]{3,2,1,0:T(8,128)(2,1)}, bf16[1,8,128,512]{3,2,1,0:T(8,128)(2,1)}, u32[]{:S(2)}, u32[]{:S(2)}) collective-permute-start(bf16[1,8,128,512]{3,2,1,0:T(8,128)(2,1)} %get-tuple-element.9), channel_id=1, source_target_pairs={{0,20},{2,22},{4,16},{6,18},{8,28},{10,30},{12,24},{14,26},{16,4},... | collective-permute-start | bytes 3145736 | tf_op jit(solution)/shard_map/ppermute | solution.py:20
  154.3 207.4 %collective-permute-start.10 = (bf16[1,8,128,512]{3,2,1,0:T(8,128)(2,1)}, bf16[1,8,128,512]{3,2,1,0:T(8,128)(2,1)S(1)}, u32[]{:S(2)}, u32[]{:S(2)}) collective-permute-start(bf16[1,8,128,512]{3,2,1,0:T(8,128)(2,1)} %get-tuple-element.8), channel_id=1, source_target_pairs={{0,22},{2,20},{4,18},{6,16},{8,30},{10,28},{12,26},{14,24},{16,6},... | collective-permute-start | bytes 3145736 | tf_op jit(solution)/shard_map/ppermute | solution.py:20
  174.4 188.4 %collective-permute-start.11 = (bf16[1,8,128,512]{3,2,1,0:T(8,128)(2,1)}, bf16[1,8,128,512]{3,2,1,0:T(8,128)(2,1)S(1)}, u32[]{:S(2)}, u32[]{:S(2)}) collective-permute-start(bf16[1,8,128,512]{3,2,1,0:T(8,128)(2,1)} %get-tuple-element.7), channel_id=1, source_target_pairs={{0,24},{2,26},{4,28},{6,30},{8,16},{10,18},{12,20},{14,22},{16,8},... | collective-permute-start | bytes 3145736 | tf_op jit(solution)/shard_map/ppermute | solution.py:20
  179.0 184.9 %collective-permute-start.12 = (bf16[1,8,128,512]{3,2,1,0:T(8,128)(2,1)S(1)}, bf16[1,8,128,512]{3,2,1,0:T(8,128)(2,1)S(1)}, u32[]{:S(2)}, u32[]{:S(2)}) collective-permute-start(bf16[1,8,128,512]{3,2,1,0:T(8,128)(2,1)S(1)} %get-tuple-element.6), channel_id=1, source_target_pairs={{0,26},{2,24},{4,30},{6,28},{8,18},{10,16},{12,22},{14,20},{16,10}... | collective-permute-start | bytes 3145736 | tf_op jit(solution)/shard_map/ppermute | solution.py:20
  272.0 93.1 %collective-permute-start.13 = (bf16[1,8,128,512]{3,2,1,0:T(8,128)(2,1)S(1)}, bf16[1,8,128,512]{3,2,1,0:T(8,128)(2,1)S(1)}, u32[]{:S(2)}, u32[]{:S(2)}) collective-permute-start(bf16[1,8,128,512]{3,2,1,0:T(8,128)(2,1)S(1)} %get-tuple-element.5), channel_id=1, source_target_pairs={{0,28},{2,30},{4,24},{6,26},{8,20},{10,22},{12,16},{14,18},{16,12}... | collective-permute-start | bytes 3145736 | tf_op jit(solution)/shard_map/ppermute | solution.py:20
  316.9 49.2 %collective-permute-start.14 = (bf16[1,8,128,512]{3,2,1,0:T(8,128)(2,1)S(1)}, bf16[1,8,128,512]{3,2,1,0:T(8,128)(2,1)S(1)}, u32[]{:S(2)}, u32[]{:S(2)}) collective-permute-start(bf16[1,8,128,512]{3,2,1,0:T(8,128)(2,1)S(1)} %get-tuple-element.4), channel_id=1, source_target_pairs={{0,30},{2,28},{4,26},{6,24},{8,22},{10,20},{12,18},{14,16},{16,14}... | collective-permute-start | bytes 3145736 | tf_op jit(solution)/shard_map/ppermute | solution.py:20
  378.6 14.2 %copy-start.3 = (s32[8,8]{1,0:T(8,128)S(1)}, s32[8,8]{1,0:T(8,128)}, u32[]{:S(2)}) copy-start(s32[8,8]{1,0:T(8,128)} %param.7) | copy-start | bytes 772
  385.8 99.8 %all-to-all-start.1 = ((bf16[2,32,128,512]{3,2,1,0:T(8,128)(2,1)}), bf16[2,32,128,512]{3,2,1,0:T(8,128)(2,1)}, u32[]{:S(2)}, u32[]{:S(2)}) async-start(bf16[2,32,128,512]{3,2,1,0:T(8,128)(2,1)} %broadcast_select_fusion.1), calls=%async_computation.1 | async-start | bytes 16777216 | tf_op jit(solution)/shard_map/all_to_all | solution.py:68
  485.6 30.7 %copy-start.4 = (f32[1,512]{1,0:T(1,128)S(1)}, f32[1,512]{1,0:T(1,128)}, u32[]{:S(2)}) copy-start(f32[1,512]{1,0:T(1,128)} %param.6) | copy-start | bytes 6148
  485.6 30.7 %copy-start.5 = (bf16[1,512,1024]{2,1,0:T(8,128)(2,1)S(1)}, bf16[1,512,1024]{2,1,0:T(8,128)(2,1)}, u32[]{:S(2)}) copy-start(bf16[1,512,1024]{2,1,0:T(8,128)(2,1)} %param.5) | copy-start | bytes 3145732
  536.7 95.2 %all-to-all-start.2 = ((f32[16,8,128]{2,1,0:T(8,128)}), f32[16,8,128]{2,1,0:T(8,128)S(1)}, u32[]{:S(2)}, u32[]{:S(2)}) async-start(f32[16,8,128]{2,1,0:T(8,128)} %get-tuple-element.21), calls=%async_computation.2 | async-start | bytes 131072 | tf_op jit(solution)/shard_map/all_to_all | solution.py:96
  631.9 10.4 %all-to-all-start.3 = ((f32[16,8,128]{2,1,0:T(8,128)}), f32[16,8,128]{2,1,0:T(8,128)S(1)}, u32[]{:S(2)}, u32[]{:S(2)}) async-start(f32[16,8,128]{2,1,0:T(8,128)} %get-tuple-element.20), calls=%async_computation.3 | async-start | bytes 131072 | tf_op jit(solution)/shard_map/all_to_all | solution.py:103
  642.9 19.8 %copy-start.2 = (f32[8,128]{1,0:T(8,128)}, f32[8,128]{1,0:T(8,128)S(1)}, u32[]{:S(2)}) copy-start(f32[8,128]{1,0:T(8,128)S(1)} %add_negate_fusion) | copy-start | bytes 12292
  644.3 10.4 %all-to-all-start.4 = ((f32[16,8,128]{2,1,0:T(8,128)}), f32[16,8,128]{2,1,0:T(8,128)S(1)}, u32[]{:S(2)}, u32[]{:S(2)}) async-start(f32[16,8,128]{2,1,0:T(8,128)} %bitcast_select_fusion), calls=%async_computation.4 | async-start | bytes 131072 | tf_op jit(solution)/shard_map/all_to_all | solution.py:121
  655.2 9.9 %copy-start.1 = (bf16[8,128,512]{2,1,0:T(8,128)(2,1)S(1)}, bf16[8,128,512]{2,1,0:T(8,128)(2,1)}, u32[]{:S(2)}) copy-start(bf16[8,128,512]{2,1,0:T(8,128)(2,1)} %param.4) | copy-start | bytes 3145732
